TPU v7x, 32 devices: a whole 2x2x4 slice. The times are simulated.
32 devices in a mesh: prompt: 4 (over x, core), sample: 8 (over z, y).
Axes of the slice: x: 2, y: 2, z: 4, core: 2. Of those that a mesh axis runs over, the one named last changes fastest.
Arguments:
- latent: bfloat16 [1024, 576], P('prompt'), may hold values from -16 to 16
- queries: bfloat16 [1024, 128, 576], P('prompt', 'sample'), may hold values from -64 to 64
- cotangent: bfloat16 [1024, 128, 512], P('prompt', 'sample'), may hold values from -18 to 18
- suffix_out: bfloat16 [1024, 128, 512], P('prompt', 'sample'), may hold values from -6 to 6
- suffix_lse: bfloat16 [1024, 128], P('prompt', 'sample'), may hold values from 6 to 10
- rewards: float32 [4], replicated, may hold values from -5 to 5
- slot_sample: int32 [1024], P('prompt'), may hold values from 0 to 4, as said below
Outputs:
- query_grad: bfloat16 [1024, 128, 576], P('prompt', 'sample')
- latent_grad: float32 [1024, 576], P('prompt')
Inputs may be any that keep to these rules, and one draw needn't show every extreme that they name: `slot_sample`: on every device the live slots come first and the others hold 4. Read over the devices in order, the live slots' completion numbers never fall, and every completion has a slot. Exactly 512 slots are live in all, and some device has all 256 of its slots live.
All inputs are finite; a program needn't handle non-finite values.
Results may differ from a plain program's by a relative error of at most 0.006.
Values may be sent and summed in bfloat16 or wider, within the bound.
A program may use at most 128 MiB of HBM per device.

v0:
```python
import math
import jax
import jax.numpy as jnp
from jax import lax
from jax.sharding import PartitionSpec as P

ROPE = 64
NOPE = 128


def softmax_scale():
    return (0.1 * math.log(40.0) + 1.0) ** 2 / math.sqrt(NOPE + ROPE)


def attend(queries, scaled, suffix_out, suffix_lse, prefix_keys, factor):
    value_width = scaled.shape[-1]
    scores = factor * jnp.einsum(
        "thd,pd->thp", queries, prefix_keys, preferred_element_type=jnp.float32
    )
    row_max = jnp.max(scores, axis=2)
    prefix_lse = row_max + jnp.log(jnp.sum(jnp.exp(scores - row_max[..., None]), axis=2))
    tail_lse = suffix_lse.astype(jnp.float32)
    joint_max = jnp.maximum(prefix_lse, tail_lse)
    total_lse = joint_max + jnp.log(jnp.exp(prefix_lse - joint_max) + jnp.exp(tail_lse - joint_max))
    probability = jnp.exp(scores - total_lse[..., None])
    prob_grad = jnp.einsum(
        "thd,pd->thp", scaled, prefix_keys[:, :value_width], preferred_element_type=jnp.float32
    )
    suffix_dot = jnp.sum(scaled.astype(jnp.float32) * suffix_out.astype(jnp.float32), axis=2)
    row_delta = (
        jnp.sum(probability * prob_grad, axis=2) + jnp.exp(tail_lse - total_lse) * suffix_dot
    )
    score_grad = (factor * probability * (prob_grad - row_delta[..., None])).astype(jnp.bfloat16)
    weights = probability.astype(jnp.bfloat16)
    query_grad = jnp.einsum(
        "thp,pd->thd", score_grad, prefix_keys, preferred_element_type=jnp.float32
    ).astype(jnp.bfloat16)

    def term_rows(first_row, row_count):
        key_term = jnp.einsum(
            "thp,thd->pd", score_grad, queries, preferred_element_type=jnp.float32
        )
        value_term = jnp.einsum("thp,thd->pd", weights, scaled, preferred_element_type=jnp.float32)
        return key_term + jnp.pad(value_term, ((0, 0), (0, key_term.shape[1] - value_width)))

    return (query_grad, term_rows)


def on_device(latent, queries, cotangent, suffix_out, suffix_lse, rewards, slot_sample):
    factor = softmax_scale()
    prefix_keys = lax.all_gather(latent, "prompt", axis=0, tiled=True)
    centred = rewards - jnp.mean(rewards)
    advantage_table = jnp.concatenate([centred, jnp.zeros((1,), jnp.float32)])
    sample_ids = jnp.arange(advantage_table.shape[0], dtype=jnp.int32)
    weight = jnp.sum(
        jnp.where(slot_sample[:, None] == sample_ids[None, :], advantage_table[None, :], 0.0),
        axis=1,
    )
    scaled = (weight[:, None, None] * cotangent.astype(jnp.float32)).astype(jnp.bfloat16)
    query_grad, term_rows = attend(queries, scaled, suffix_out, suffix_lse, prefix_keys, factor)
    prefix_count = prefix_keys.shape[0]
    owner_sums = lax.psum_scatter(
        term_rows(0, prefix_count), "prompt", scatter_dimension=0, tiled=True
    )
    latent_grad = lax.psum(owner_sums, "sample")
    return (query_grad, latent_grad)


def solution(mesh):
    in_specs = (
        P("prompt", None),
        P("prompt", "sample", None),
        P("prompt", "sample", None),
        P("prompt", "sample", None),
        P("prompt", "sample"),
        P(),
        P("prompt"),
    )
    out_specs = (P("prompt", "sample", None), P("prompt", None))
    return jax.shard_map(
        on_device, mesh=mesh, in_specs=in_specs, out_specs=out_specs, check_vma=False
    )
```

profile of v0, /device:TPU:0, one launch (start us, length us, event | category | flops | bytes accessed | tf_op | source)
XLA Modules:
  0.0 206.3 jit_solution(13262518655812535774)
XLA Ops:
  7.2 0.0 all-gather.2.cloned.1.call-start
  7.2 0.7 all-gather.2.cloned.1.call-update
  7.9 0.0 reduce-scatter.2.cloned.1.call-start
  7.9 1.3 reduce_sum.46
  9.9 0.7 broadcast_subtract_fusion
  10.5 0.1 pad_maximum_fusion
  10.6 0.8 select_reduce_fusion
  11.4 6.0 %multiply_reduce_fusion.2 = (f32[256,16]{1,0:T(8,128)S(1)}, bf16[256,16,512]{2,1,0:T(8,128)(2,1)}) fusion(bf16[256,16,512]{2,1,0:T(8,128)(2,1)} %param.10, bf16[256,16,512]{2,1,0:T(8,128)(2,1)} %param.9, f32[256]{0:T(256)S(1)} %select_reduce_fusion), kind=kLoop, calls=%fused_computation.7 | loop fusion | flops 14675968 | bytes 12600320 | tf_op jit(solution)/shard_map/reduce_sum | solution.py:29
  17.3 0.1 copy.25
  17.4 7.6 %copy.26 = bf16[256,16,512]{0,2,1:T(8,128)(2,1)} copy(bf16[256,16,512]{2,1,0:T(8,128)(2,1)} %get-tuple-element.3) | data formatting | bytes 8388608 | tf_op jit(solution)/shard_map/convert_element_type | solution.py:59
  25.0 4.9 %all-gather.2.cloned.1.call-done = bf16[1024,576]{0,1:T(8,128)(2,1)} async-done(((bf16[256,576]{0,1:T(8,128)(2,1)}), bf16[1024,576]{0,1:T(8,128)(2,1)}) %all-gather.2.cloned.1.call-update) | async-done | bytes 1179664 | tf_op jit(solution)/shard_map/all_gather | solution.py:51
  29.8 9.1 %multiply_reduce_fusion.1 = (f32[256,16]{0,1:T(8,128)S(1)}, f32[256,16,1024]{2,0,1:T(8,128)S(1)}) fusion(bf16[256,16,576]{0,2,1:T(8,128)(2,1)} %param.8, bf16[1024,576]{0,1:T(8,128)(2,1)} %all-gather.2.cloned.1.call-done), kind=kOutput, calls=%fused_computation.4 | convolution fusion | flops 4840222720 | bytes 22691840 | tf_op jit(solution)/shard_map/thd,pd->thp/dot_general | solution.py:17
  39.0 3.7 %exponential_reduce_fusion = f32[256,16]{0,1:T(8,128)S(1)} fusion(f32[256,16,1024]{2,0,1:T(8,128)S(1)} %get-tuple-element.5, f32[256,16]{0,1:T(8,128)S(1)} %get-tuple-element.4), kind=kLoop, calls=%fused_computation.3 | loop fusion | flops 12578816 | bytes 16809984 | tf_op jit(solution)/shard_map/reduce_sum | solution.py:21
  42.8 3.3 %copy-done = f32[256,16,1024]{2,0,1:T(8,128)} copy-done((f32[256,16,1024]{2,0,1:T(8,128)}, f32[256,16,1024]{2,0,1:T(8,128)S(1)}, u32[]{:S(2)}) %copy-start) | copy-done | bytes 16777240
  46.1 6.2 %fusion.5 = f32[1024,512]{0,1:T(8,128)} fusion(bf16[256,16,512]{0,2,1:T(8,128)(2,1)S(1)} %copy-done.1, f32[256,16,1024]{2,0,1:T(8,128)S(1)} %get-tuple-element.5, f32[256,16]{0,1:T(8,128)S(1)} %fusion.12), kind=kOutput, calls=%fused_computation.13 | convolution fusion | flops 4307550208 | bytes 23085056 | tf_op jit(solution)/shard_map/thp,thd->pd/dot_general | solution.py:43
  52.3 13.5 %multiply_reduce_fusion = (f32[256,16]{0,1:T(8,128)S(1)}, f32[256,16,1024]{2,0,1:T(8,128)}) fusion(f32[256,16,1024]{2,0,1:T(8,128)} %copy-done, f32[256,16]{0,1:T(8,128)S(1)} %fusion.12, bf16[256,16,512]{0,2,1:T(8,128)(2,1)S(1)} %copy-done.1, bf16[1024,576]{0,1:T(8,128)(2,1)S(1)} %copy-done.3), kind=kOutput, calls=%fused_computation.1 | convolution fusion | flops 4311740416 | bytes 38830080 | tf_op jit(solution)/shard_map/thd,pd->thp/dot_general | solution.py:26
  65.8 12.7 %multiply_convert_fusion = bf16[256,16,1024]{2,0,1:T(8,128)(2,1)S(1)} fusion(f32[256,16,1024]{2,0,1:T(8,128)} %get-tuple-element.7, f32[256,16,1024]{2,0,1:T(8,128)} %copy-done, f32[256,16]{0,1:T(8,128)S(1)} %fusion.20, f32[256,16]{0,1:T(8,128)S(1)} %fusion.12), kind=kLoop, calls=%fused_computation | loop fusion | flops 25165824 | bytes 41975808 | tf_op jit(solution)/shard_map/convert_element_type | solution.py:33
  78.6 3.2 %copy-done.2 = bf16[256,16,1024]{2,0,1:T(8,128)(2,1)} copy-done((bf16[256,16,1024]{2,0,1:T(8,128)(2,1)}, bf16[256,16,1024]{2,0,1:T(8,128)(2,1)S(1)}, u32[]{:S(2)}) %copy-start.2) | copy-done | bytes 8388632
  81.8 6.5 %bitcast_add_fusion = f32[1024,576]{0,1:T(8,128)} fusion(f32[1024,512]{0,1:T(8,128)S(1)} %copy-done.5, bf16[256,16,576]{0,2,1:T(8,128)(2,1)S(1)} %bitcast.23, bf16[256,16,1024]{2,0,1:T(8,128)(2,1)S(1)} %multiply_convert_fusion), kind=kOutput, calls=%fused_computation.12 | convolution fusion | flops 4832428032 | bytes 17563648 | tf_op jit(solution)/shard_map/thp,thd->pd/dot_general | solution.py:40
  88.3 0.0 all-reduce.3.cloned.1.call-start
  88.4 32.9 %reduce-scatter.2.cloned.1.call-done = f32[256,576]{0,1:T(8,128)} async-done(((f32[1024,576]{0,1:T(8,128)}), f32[256,576]{0,1:T(8,128)}) %reduce-scatter.2.cloned.1.call-update) | async-done | bytes 589840 | tf_op jit(solution)/shard_map/reduce_scatter | solution.py:62
  121.3 10.1 %convolution_convert_fusion = bf16[256,16,576]{0,2,1:T(8,128)(2,1)} fusion(bf16[256,16,1024]{2,0,1:T(8,128)(2,1)} %copy-done.2, bf16[1024,576]{0,1:T(8,128)(2,1)S(1)} %copy-done.3), kind=kOutput, calls=%fused_computation.11 | convolution fusion | flops 4834197504 | bytes 14286848 | tf_op jit(solution)/shard_map/thp,pd->thd/dot_general | solution.py:35
  131.4 66.5 %all-reduce.3.cloned.1.call-done = f32[256,576]{0,1:T(8,128)} async-done(((f32[256,576]{0,1:T(8,128)}), f32[256,576]{0,1:T(8,128)}) %all-reduce.3.cloned.1.call-update) | async-done | bytes 589840 | tf_op jit(solution)/shard_map/psum | solution.py:65
  197.9 1.9 copy.30
  (19 shorter events, 0.1 us)
Async XLA Ops:
  7.2 22.7 %all-gather.2.cloned.1.call-start = ((), (), s32[]{:S(2)}) async-start(), calls=%async_computation.1 | async-start | bytes 1474560 | tf_op jit(solution)/shard_map/all_gather | solution.py:51
  7.9 113.4 %reduce-scatter.2.cloned.1.call-start = ((), (), s32[]{:S(2)}) async-start(), calls=%async_computation.2 | async-start | bytes 2949120 | tf_op jit(solution)/shard_map/reduce_scatter | solution.py:62
  39.0 7.1 %copy-start = (f32[256,16,1024]{2,0,1:T(8,128)}, f32[256,16,1024]{2,0,1:T(8,128)S(1)}, u32[]{:S(2)}) copy-start(f32[256,16,1024]{2,0,1:T(8,128)S(1)} %get-tuple-element.5) | copy-start | bytes 50331652
  39.0 3.7 %copy-start.4 = (bf16[256,16]{0,1:T(8,128)(2,1)S(1)}, bf16[256,16]{0,1:T(8,128)(2,1)}, u32[]{:S(2)}) copy-start(bf16[256,16]{0,1:T(8,128)(2,1)} %param.11) | copy-start | bytes 24580
  39.0 7.1 %copy-start.1 = (bf16[256,16,512]{0,2,1:T(8,128)(2,1)S(1)}, bf16[256,16,512]{0,2,1:T(8,128)(2,1)}, u32[]{:S(2)}) copy-start(bf16[256,16,512]{0,2,1:T(8,128)(2,1)} %copy.26) | copy-start | bytes 12582916
  46.1 6.2 %copy-start.3 = (bf16[1024,576]{0,1:T(8,128)(2,1)S(1)}, bf16[1024,576]{0,1:T(8,128)(2,1)}, u32[]{:S(2)}) copy-start(bf16[1024,576]{0,1:T(8,128)(2,1)} %all-gather.2.cloned.1.call-done) | copy-start | bytes 3538948
  52.3 29.5 %slice-start = ((s8[4718592]{0:T(1024)(128)(4,1)}), s8[524288]{0:T(1024)(128)(4,1)S(1)}, s32[]{:S(2)}) async-start(s8[4718592]{0:T(1024)(128)(4,1)} %bitcast.22), calls=%async_computation.4 | async-start | bytes 1048576
  65.8 16.0 %slice-start.1 = ((s8[4718592]{0:T(1024)(128)(4,1)}), s8[4194304]{0:T(1024)(128)(4,1)S(1)}, s32[]{:S(2)}) async-start(s8[4718592]{0:T(1024)(128)(4,1)} %bitcast.22), calls=%async_computation.5 | async-start | bytes 8388608
  65.8 16.0 %copy-start.5 = (f32[1024,512]{0,1:T(8,128)S(1)}, f32[1024,512]{0,1:T(8,128)}, u32[]{:S(2)}) copy-start(f32[1024,512]{0,1:T(8,128)} %fusion.5) | copy-start | bytes 6291460
  78.6 3.2 %copy-start.2 = (bf16[256,16,1024]{2,0,1:T(8,128)(2,1)}, bf16[256,16,1024]{2,0,1:T(8,128)(2,1)S(1)}, u32[]{:S(2)}) copy-start(bf16[256,16,1024]{2,0,1:T(8,128)(2,1)S(1)} %multiply_convert_fusion) | copy-start | bytes 25165828
  88.3 109.6 %all-reduce.3.cloned.1.call-start = ((), (), s32[]{:S(2)}) async-start(), calls=%async_computation.3 | async-start | bytes 1179648 | tf_op jit(solution)/shard_map/psum | solution.py:65
Sparse Core Ops, SparseCore 0:
  9.5 20.2 all-gather.1
  88.4 32.7 reduce-scatter.1
  124.6 73.2 all-reduce.2
where the time goes:
time: 207 us; the launch traced here: 206 us
  waiting for transfers between devices  105 us (51%)
  matrix products  45.4 us (22%)
  other arithmetic  25.2 us (12%)
  local copies, waits for them, and re-layouts  16.1 us (8%)
  between operations  14.5 us (7%)
    psum x1, waiting for transfers between devices, on_device(): latent_grad = lax.psum(owner_sums, 'sample')  66.5 us
    reduce_scatter x1, waiting for transfers between devices, on_device(): lax.psum_scatter(term_rows(0, prefix_count), 'prompt', scatter_dimension=...  32.9 us
    dot_general x1, matrix products, attend(): jnp.einsum('thd,pd->thp', scaled, prefix_keys[:, :value_width], preferred...  13.5 us
    convert_element_type x1, other arithmetic, attend(): (factor * probability * (prob_grad - row_delta[..., None])).astype(jnp.bf...  12.7 us
    dot_general x1, matrix products, attend(): jnp.einsum('thp,pd->thd', score_grad, prefix_keys, preferred_element_type...  10.1 us
    dot_general x1, matrix products, attend(): jnp.einsum('thd,pd->thp', queries, prefix_keys, preferred_element_type=jn...  9.15 us
    unnamed x17, local copies, waits for them, and re-layouts  8.49 us
    convert_element_type x1, local copies, waits for them, and re-layouts, on_device(): (weight[:, None, None] * cotangent.astype(jnp.float32)).astype(jnp.bfloat16)  7.59 us
  transfers between devices with their start and end apart: 3, of which 3 were waited for; matrix products, arithmetic and copies ran while one was open for 13% of the time, Pallas kernels for 0%

commit v1 on v0

--- a/solution.py
+++ b/solution.py
@@ -62,7 +62,10 @@
     owner_sums = lax.psum_scatter(
         term_rows(0, prefix_count), "prompt", scatter_dimension=0, tiled=True
     )
-    latent_grad = lax.psum(owner_sums, "sample")
+    size, latent_grad = (lax.axis_size("sample"), owner_sums)
+    for far in [1 << k for k in range(size.bit_length() - 1)]:
+        route = [(i, i ^ far) for i in range(size)]
+        latent_grad = latent_grad + lax.ppermute(latent_grad, "sample", route)
     return (query_grad, latent_grad)
 
 

time: 207 us -> 187 us (0.903)
  waiting for transfers between devices: 105 us -> 79 us
  starting transfers between devices: 0.12 us -> 5.54 us
  other arithmetic: 25.2 us -> 27.3 us
    psum x1 -> x0, waiting for transfers between devices: 66.5 us -> none  [on_device(): latent_grad = lax.psum(owner_sums, 'sample')]
    ppermute x0 -> x3, waiting for transfers between devices: none -> 40.5 us  [on_device(): latent_grad = latent_grad + lax.ppermute(latent_grad, 'sample', route)]
    ppermute x0 -> x3, starting transfers between devices: none -> 5.46 us  [on_device(): latent_grad = latent_grad + lax.ppermute(latent_grad, 'sample', route)]
    add x0 -> x3, other arithmetic: none -> 2.11 us  [on_device(): latent_grad = latent_grad + lax.ppermute(latent_grad, 'sample', route)]
    unnamed x17 -> x16, local copies, waits for them, and re-layouts: 8.49 us -> 6.56 us
  transfers between devices with their start and end apart: 3 -> 5, of which waited for: 3 -> 5; matrix products, arithmetic and copies ran while one was open for 13% -> 14% of each run, Pallas kernels for 0% -> 0%
where the time goes in v1:
time: 187 us; the launch traced here: 186 us
  waiting for transfers between devices  79 us (42%)
  matrix products  45.4 us (24%)
  other arithmetic  27.3 us (15%)
  between operations  14.8 us (8%)
  local copies, waits for them, and re-layouts  14.2 us (8%)
  starting transfers between devices  5.54 us (3%)
    ppermute x3, waiting for transfers between devices, on_device(): latent_grad = latent_grad + lax.ppermute(latent_grad, 'sample', route)  40.5 us
    reduce_scatter x1, waiting for transfers between devices, on_device(): lax.psum_scatter(term_rows(0, prefix_count), 'prompt', scatter_dimension=...  32.9 us
    dot_general x1, matrix products, attend(): jnp.einsum('thd,pd->thp', scaled, prefix_keys[:, :value_width], preferred...  13.5 us
    convert_element_type x1, other arithmetic, attend(): (factor * probability * (prob_grad - row_delta[..., None])).astype(jnp.bf...  12.7 us
    dot_general x1, matrix products, attend(): jnp.einsum('thp,pd->thd', score_grad, prefix_keys, preferred_element_type...  10.1 us
    dot_general x1, matrix products, attend(): jnp.einsum('thd,pd->thp', queries, prefix_keys, preferred_element_type=jn...  9.15 us
    convert_element_type x1, local copies, waits for them, and re-layouts, on_device(): (weight[:, None, None] * cotangent.astype(jnp.float32)).astype(jnp.bfloat16)  7.56 us
    unnamed x16, local copies, waits for them, and re-layouts  6.56 us
  transfers between devices with their start and end apart: 5, of which 5 were waited for; matrix products, arithmetic and copies ran while one was open for 14% of the time, Pallas kernels for 0%

profile of v1, /device:TPU:0, one launch (start us, length us, event | category | flops | bytes accessed | tf_op | source)
XLA Modules:
  0.0 186.2 jit_solution(14437693251459643378)
XLA Ops:
  7.2 0.7 all-gather.2.cloned.1.call-update
  7.9 1.3 reduce_sum.46
  10.6 0.8 select_reduce_fusion
  11.4 6.0 %multiply_reduce_fusion.2 = (f32[256,16]{1,0:T(8,128)S(1)}, bf16[256,16,512]{2,1,0:T(8,128)(2,1)}) fusion(bf16[256,16,512]{2,1,0:T(8,128)(2,1)} %param.10, bf16[256,16,512]{2,1,0:T(8,128)(2,1)} %param.9, f32[256]{0:T(256)S(1)} %select_reduce_fusion), kind=kLoop, calls=%fused_computation.7 | loop fusion | flops 14675968 | bytes 12600320 | tf_op jit(solution)/shard_map/reduce_sum | solution.py:29
  17.4 7.6 %copy.26 = bf16[256,16,512]{0,2,1:T(8,128)(2,1)} copy(bf16[256,16,512]{2,1,0:T(8,128)(2,1)} %get-tuple-element.3) | data formatting | bytes 8388608 | tf_op jit(solution)/shard_map/convert_element_type | solution.py:59
  24.9 4.9 %all-gather.2.cloned.1.call-done = bf16[1024,576]{0,1:T(8,128)(2,1)} async-done(((bf16[256,576]{0,1:T(8,128)(2,1)}), bf16[1024,576]{0,1:T(8,128)(2,1)}) %all-gather.2.cloned.1.call-update) | async-done | bytes 1179664 | tf_op jit(solution)/shard_map/all_gather | solution.py:51
  29.8 9.1 %multiply_reduce_fusion.1 = (f32[256,16]{0,1:T(8,128)S(1)}, f32[256,16,1024]{2,0,1:T(8,128)S(1)}) fusion(bf16[256,16,576]{0,2,1:T(8,128)(2,1)} %param.8, bf16[1024,576]{0,1:T(8,128)(2,1)} %all-gather.2.cloned.1.call-done), kind=kOutput, calls=%fused_computation.4 | convolution fusion | flops 4840222720 | bytes 22691840 | tf_op jit(solution)/shard_map/thd,pd->thp/dot_general | solution.py:17
  39.0 3.7 %exponential_reduce_fusion = f32[256,16]{0,1:T(8,128)S(1)} fusion(f32[256,16,1024]{2,0,1:T(8,128)S(1)} %get-tuple-element.5, f32[256,16]{0,1:T(8,128)S(1)} %get-tuple-element.4), kind=kLoop, calls=%fused_computation.3 | loop fusion | flops 12578816 | bytes 16809984 | tf_op jit(solution)/shard_map/reduce_sum | solution.py:21
  42.8 3.3 %copy-done = f32[256,16,1024]{2,0,1:T(8,128)} copy-done((f32[256,16,1024]{2,0,1:T(8,128)}, f32[256,16,1024]{2,0,1:T(8,128)S(1)}, u32[]{:S(2)}) %copy-start) | copy-done | bytes 16777240
  46.1 6.2 %fusion.5 = f32[1024,512]{0,1:T(8,128)} fusion(bf16[256,16,512]{0,2,1:T(8,128)(2,1)S(1)} %copy-done.1, f32[256,16,1024]{2,0,1:T(8,128)S(1)} %get-tuple-element.5, f32[256,16]{0,1:T(8,128)S(1)} %fusion.12), kind=kOutput, calls=%fused_computation.13 | convolution fusion | flops 4307550208 | bytes 23085056 | tf_op jit(solution)/shard_map/thp,thd->pd/dot_general | solution.py:43
  52.3 13.5 %multiply_reduce_fusion = (f32[256,16]{0,1:T(8,128)S(1)}, f32[256,16,1024]{2,0,1:T(8,128)}) fusion(f32[256,16,1024]{2,0,1:T(8,128)} %copy-done, f32[256,16]{0,1:T(8,128)S(1)} %fusion.12, bf16[256,16,512]{0,2,1:T(8,128)(2,1)S(1)} %copy-done.1, bf16[1024,576]{0,1:T(8,128)(2,1)S(1)} %copy-done.3), kind=kOutput, calls=%fused_computation.1 | convolution fusion | flops 4311740416 | bytes 38830080 | tf_op jit(solution)/shard_map/thd,pd->thp/dot_general | solution.py:26
  65.8 12.7 %multiply_convert_fusion = bf16[256,16,1024]{2,0,1:T(8,128)(2,1)S(1)} fusion(f32[256,16,1024]{2,0,1:T(8,128)} %get-tuple-element.7, f32[256,16,1024]{2,0,1:T(8,128)} %copy-done, f32[256,16]{0,1:T(8,128)S(1)} %fusion.20, f32[256,16]{0,1:T(8,128)S(1)} %fusion.12), kind=kLoop, calls=%fused_computation | loop fusion | flops 25165824 | bytes 41975808 | tf_op jit(solution)/shard_map/convert_element_type | solution.py:33
  78.5 3.2 %copy-done.2 = bf16[256,16,1024]{2,0,1:T(8,128)(2,1)} copy-done((bf16[256,16,1024]{2,0,1:T(8,128)(2,1)}, bf16[256,16,1024]{2,0,1:T(8,128)(2,1)S(1)}, u32[]{:S(2)}) %copy-start.2) | copy-done | bytes 8388632
  81.8 6.5 %bitcast_add_fusion = f32[1024,576]{0,1:T(8,128)} fusion(f32[1024,512]{0,1:T(8,128)S(1)} %copy-done.5, bf16[256,16,576]{0,2,1:T(8,128)(2,1)S(1)} %bitcast.23, bf16[256,16,1024]{2,0,1:T(8,128)(2,1)S(1)} %multiply_convert_fusion), kind=kOutput, calls=%fused_computation.12 | convolution fusion | flops 4832428032 | bytes 17563648 | tf_op jit(solution)/shard_map/thp,thd->pd/dot_general | solution.py:40
  88.3 32.9 %reduce-scatter.2.cloned.1.call-done = f32[256,576]{0,1:T(8,128)} async-done(((f32[1024,576]{0,1:T(8,128)}), f32[256,576]{0,1:T(8,128)}) %reduce-scatter.2.cloned.1.call-update) | async-done | bytes 589840 | tf_op jit(solution)/shard_map/reduce_scatter | solution.py:62
  121.2 1.5 collective-permute-start
  122.7 13.6 %collective-permute-done = f32[256,576]{0,1:T(8,128)S(1)} collective-permute-done((f32[256,576]{0,1:T(8,128)}, f32[256,576]{0,1:T(8,128)S(1)}, u32[]{:S(2)}, u32[]{:S(2)}) %collective-permute-start) | collective-permute-done | bytes 589856 | tf_op jit(solution)/shard_map/ppermute | solution.py:68
  136.3 1.1 add.33
  137.5 1.6 collective-permute-start.1
  139.0 12.6 %collective-permute-done.1 = f32[256,576]{0,1:T(8,128)S(1)} collective-permute-done((f32[256,576]{0,1:T(8,128)S(1)}, f32[256,576]{0,1:T(8,128)S(1)}, u32[]{:S(2)}, u32[]{:S(2)}) %collective-permute-start.1) | collective-permute-done | bytes 589856 | tf_op jit(solution)/shard_map/ppermute | solution.py:68
  151.7 2.4 %collective-permute-start.2 = (f32[256,576]{0,1:T(8,128)S(1)}, f32[256,576]{0,1:T(8,128)S(1)}, u32[]{:S(2)}, u32[]{:S(2)}) collective-permute-start(f32[256,576]{0,1:T(8,128)S(1)} %add.34), channel_id=1, source_target_pairs={{0,4},{1,5},{2,6},{3,7},{4,0},{5,1},{6,2},{7,3},{8,12},{9,13},{10,... | collective-permute-start | bytes 1769480 | tf_op jit(solution)/shard_map/ppermute | solution.py:68
  154.1 10.1 %convolution_convert_fusion = bf16[256,16,576]{0,2,1:T(8,128)(2,1)} fusion(bf16[256,16,1024]{2,0,1:T(8,128)(2,1)} %copy-done.2, bf16[1024,576]{0,1:T(8,128)(2,1)S(1)} %copy-done.3), kind=kOutput, calls=%fused_computation.11 | convolution fusion | flops 4834197504 | bytes 14286848 | tf_op jit(solution)/shard_map/thp,pd->thd/dot_general | solution.py:35
  164.2 14.3 %collective-permute-done.2 = f32[256,576]{0,1:T(8,128)S(1)} collective-permute-done((f32[256,576]{0,1:T(8,128)S(1)}, f32[256,576]{0,1:T(8,128)S(1)}, u32[]{:S(2)}, u32[]{:S(2)}) %collective-permute-start.2) | collective-permute-done | bytes 589856 | tf_op jit(solution)/shard_map/ppermute | solution.py:68
  178.5 0.9 add.35
  (24 shorter events, 1.0 us)
Async XLA Ops:
  7.2 22.7 %all-gather.2.cloned.1.call-start = ((), (), s32[]{:S(2)}) async-start(), calls=%async_computation.1 | async-start | bytes 1474560 | tf_op jit(solution)/shard_map/all_gather | solution.py:51
  7.9 113.3 %reduce-scatter.2.cloned.1.call-start = ((), (), s32[]{:S(2)}) async-start(), calls=%async_computation.2 | async-start | bytes 2949120 | tf_op jit(solution)/shard_map/reduce_scatter | solution.py:62
  39.0 7.1 %copy-start = (f32[256,16,1024]{2,0,1:T(8,128)}, f32[256,16,1024]{2,0,1:T(8,128)S(1)}, u32[]{:S(2)}) copy-start(f32[256,16,1024]{2,0,1:T(8,128)S(1)} %get-tuple-element.5) | copy-start | bytes 50331652
  39.0 3.7 %copy-start.4 = (bf16[256,16]{0,1:T(8,128)(2,1)S(1)}, bf16[256,16]{0,1:T(8,128)(2,1)}, u32[]{:S(2)}) copy-start(bf16[256,16]{0,1:T(8,128)(2,1)} %param.11) | copy-start | bytes 24580
  39.0 7.1 %copy-start.1 = (bf16[256,16,512]{0,2,1:T(8,128)(2,1)S(1)}, bf16[256,16,512]{0,2,1:T(8,128)(2,1)}, u32[]{:S(2)}) copy-start(bf16[256,16,512]{0,2,1:T(8,128)(2,1)} %copy.26) | copy-start | bytes 12582916
  46.1 6.2 %copy-start.3 = (bf16[1024,576]{0,1:T(8,128)(2,1)S(1)}, bf16[1024,576]{0,1:T(8,128)(2,1)}, u32[]{:S(2)}) copy-start(bf16[1024,576]{0,1:T(8,128)(2,1)} %all-gather.2.cloned.1.call-done) | copy-start | bytes 3538948
  52.3 29.5 %slice-start = ((s8[4718592]{0:T(1024)(128)(4,1)}), s8[524288]{0:T(1024)(128)(4,1)S(1)}, s32[]{:S(2)}) async-start(s8[4718592]{0:T(1024)(128)(4,1)} %bitcast.22), calls=%async_computation.3 | async-start | bytes 1048576
  65.8 16.0 %slice-start.1 = ((s8[4718592]{0:T(1024)(128)(4,1)}), s8[4194304]{0:T(1024)(128)(4,1)S(1)}, s32[]{:S(2)}) async-start(s8[4718592]{0:T(1024)(128)(4,1)} %bitcast.22), calls=%async_computation.4 | async-start | bytes 8388608
  65.8 16.0 %copy-start.5 = (f32[1024,512]{0,1:T(8,128)S(1)}, f32[1024,512]{0,1:T(8,128)}, u32[]{:S(2)}) copy-start(f32[1024,512]{0,1:T(8,128)} %fusion.5) | copy-start | bytes 6291460
  78.5 3.2 %copy-start.2 = (bf16[256,16,1024]{2,0,1:T(8,128)(2,1)}, bf16[256,16,1024]{2,0,1:T(8,128)(2,1)S(1)}, u32[]{:S(2)}) copy-start(bf16[256,16,1024]{2,0,1:T(8,128)(2,1)S(1)} %multiply_convert_fusion) | copy-start | bytes 25165828
  121.2 15.1 %collective-permute-start = (f32[256,576]{0,1:T(8,128)}, f32[256,576]{0,1:T(8,128)S(1)}, u32[]{:S(2)}, u32[]{:S(2)}) collective-permute-start(f32[256,576]{0,1:T(8,128)} %reduce-scatter.2.cloned.1.call-done), channel_id=1, source_target_pairs={{0,1},{1,0},{2,3},{3,2},{4,5},{5,4},{6,7},{7,6},{8,9},{9,8},{10,11... | collective-permute-start | bytes 1769480 | tf_op jit(solution)/shard_map/ppermute | solution.py:68
  137.5 14.1 %collective-permute-start.1 = (f32[256,576]{0,1:T(8,128)S(1)}, f32[256,576]{0,1:T(8,128)S(1)}, u32[]{:S(2)}, u32[]{:S(2)}) collective-permute-start(f32[256,576]{0,1:T(8,128)S(1)} %add.33), channel_id=1, source_target_pairs={{0,2},{1,3},{2,0},{3,1},{4,6},{5,7},{6,4},{7,5},{8,10},{9,11},{10,... | collective-permute-start | bytes 1769480 | tf_op jit(solution)/shard_map/ppermute | solution.py:68
  151.7 26.8 %collective-permute-start.2 = (f32[256,576]{0,1:T(8,128)S(1)}, f32[256,576]{0,1:T(8,128)S(1)}, u32[]{:S(2)}, u32[]{:S(2)}) collective-permute-start(f32[256,576]{0,1:T(8,128)S(1)} %add.34), channel_id=1, source_target_pairs={{0,4},{1,5},{2,6},{3,7},{4,0},{5,1},{6,2},{7,3},{8,12},{9,13},{10,... | collective-permute-start | bytes 1769480 | tf_op jit(solution)/shard_map/ppermute | solution.py:68
Sparse Core Ops, SparseCore 0:
  9.5 20.2 all-gather.1
  88.4 32.7 reduce-scatter.1
